TPU v7x, 128 devices: a whole 4x4x4 slice. The times are simulated.
128 devices in a mesh: req: 16 (over x, z), kv: 8 (over y, core).
Axes of the slice: x: 4, y: 4, z: 4, core: 2. Of those that a mesh axis runs over, the one named last changes fastest.
Arguments:
- residual_in: bfloat16 [512, 4096], P(None, 'req'), may hold values from -6 to 6
- attn_gain: float32 [4096], replicated, may hold values from 0.1 to 1.9
- query_weight: bfloat16 [4096, 4096], P(None, 'kv'), may hold values from -0.09375 to 0.09375
- key_matrix: bfloat16 [4096, 1024], P(None, 'kv'), may hold values from -0.09375 to 0.09375
- value_matrix: bfloat16 [4096, 1024], P(None, 'kv'), may hold values from -0.09375 to 0.09375
- key_cache: bfloat16 [512, 8, 640, 128], P('req', 'kv'), may hold values from -400 to 400
- cached_values: bfloat16 [512, 8, 640, 128], P('req', 'kv'), may hold values from -6 to 6
- cache_lengths: int32 [512], P('req'), may hold values from 1 to 640, as said below
- positions: int32 [512], P('req'), may hold values from 640 to 16383
- output_weight: bfloat16 [4096, 4096], P(None, 'req'), may hold values from -0.09375 to 0.09375
- mlp_gain: float32 [4096], P('req'), may hold values from 0.1 to 1.9
- gate_weight: bfloat16 [4096, 14336], P('req', 'kv'), may hold values from -0.09375 to 0.09375
- up_weight: bfloat16 [4096, 14336], P('req', 'kv'), may hold values from -0.09375 to 0.09375
- down_weight: bfloat16 [14336, 4096], P('kv', 'req'), may hold values from -0.046875 to 0.046875
Outputs:
- output: bfloat16 [512, 4096], P('kv', 'req')
Inputs may be any that keep to these rules, and one draw needn't show every extreme that they name: `cache_lengths`: each request's filled slots; some request has exactly 640 and some exactly 1.
All inputs are finite; a program needn't handle non-finite values.
Results may differ from a plain program's by a relative error of at most 0.025.
Values may be sent and summed in bfloat16 or wider, within the bound.
A program may use at most 128 MiB of HBM per device.

v0:
```python
import math
import jax
import jax.numpy as jnp
from jax import lax
from jax.sharding import PartitionSpec as P

MODEL_WIDTH = 4096
WINDOW = 512
SINKS = 4
EPS = 1e-05
THETA = 10000.0


def apply_rotary(vectors, places):
    half = vectors.shape[-1] // 2
    freqs = jnp.exp(
        jnp.arange(half, dtype=jnp.float32) * (-2.0 * math.log(THETA) / vectors.shape[-1])
    )
    angles = places.astype(jnp.float32)[:, None] * freqs[None, :]
    cosine = jnp.cos(angles)[:, None, :]
    sine = jnp.sin(angles)[:, None, :]
    first = vectors[..., :half]
    second = vectors[..., half:]
    return jnp.concatenate(
        [first * cosine - second * sine, second * cosine + first * sine], axis=-1
    )


def attend(query_rows, keys, values, new_key, new_value, allowed):
    factor = 1.0 / math.sqrt(query_rows.shape[-1])
    scores = (
        jnp.einsum("bgd,bjd->bgj", query_rows, keys, preferred_element_type=jnp.float32) * factor
    )
    scores = jnp.where(allowed[:, None, :], scores, -1e30)
    own = jnp.einsum("bgd,bd->bg", query_rows, new_key, preferred_element_type=jnp.float32) * factor
    peak = jnp.maximum(jnp.max(scores, axis=-1), own)
    expo = jnp.where(allowed[:, None, :], jnp.exp(scores - peak[..., None]), 0.0)
    own_expo = jnp.exp(own - peak)
    denom = jnp.sum(expo, axis=-1) + own_expo
    weights = (expo / denom[..., None]).astype(jnp.bfloat16)
    own_weight = (own_expo / denom).astype(jnp.bfloat16)
    mixed = jnp.einsum("bgj,bjd->bgd", weights, values, preferred_element_type=jnp.float32)
    mixed = (
        mixed
        + own_weight.astype(jnp.float32)[..., None] * new_value.astype(jnp.float32)[:, None, :]
    )
    return mixed.astype(jnp.bfloat16)


def shards(
    residual_in,
    attn_gain,
    query_weight,
    key_matrix,
    value_matrix,
    key_cache,
    cached_values,
    cache_lengths,
    positions,
    output_weight,
    mlp_gain,
    gate_weight,
    up_weight,
    down_weight,
):
    tokens = lax.all_to_all(residual_in, "req", split_axis=0, concat_axis=1, tiled=True)
    local_rows = tokens.shape[0]
    heads_here = key_cache.shape[1]
    head_size = key_cache.shape[3]
    query_group = query_weight.shape[1] // (heads_here * head_size)
    stream = tokens.astype(jnp.float32)
    normed_input = (
        stream
        / jnp.sqrt(jnp.sum(stream * stream, axis=-1, keepdims=True) / MODEL_WIDTH + EPS)
        * attn_gain
    ).astype(jnp.bfloat16)
    query_rows = jnp.dot(normed_input, query_weight, preferred_element_type=jnp.float32).reshape(
        local_rows, heads_here * query_group, head_size
    )
    query_rows = (
        apply_rotary(query_rows, positions)
        .astype(jnp.bfloat16)
        .reshape(local_rows, heads_here, query_group, head_size)
    )
    fresh_keys = jnp.dot(normed_input, key_matrix, preferred_element_type=jnp.float32).reshape(
        local_rows, heads_here, head_size
    )
    fresh_keys = apply_rotary(fresh_keys, positions).astype(jnp.bfloat16)
    fresh_values = (
        jnp.dot(normed_input, value_matrix, preferred_element_type=jnp.float32)
        .reshape(local_rows, heads_here, head_size)
        .astype(jnp.bfloat16)
    )
    slots = jnp.arange(key_cache.shape[2], dtype=jnp.int32)[None, :]
    limit = cache_lengths[:, None]
    allowed = (slots < limit) & ((slots < SINKS) | (slots > limit - WINDOW))
    results = [
        attend(
            query_rows[:, 0],
            key_cache[:, 0],
            cached_values[:, 0],
            fresh_keys[:, 0],
            fresh_values[:, 0],
            allowed,
        )
    ]
    attended_rows = jnp.stack(results, axis=1).reshape(
        local_rows, heads_here * query_group * head_size
    )
    features = attended_rows.shape[1]
    kv_place = lax.axis_index("kv")
    weight_rows = lax.dynamic_slice_in_dim(output_weight, kv_place * features, features, 0)
    partial_mix = jnp.dot(
        lax.all_gather(attended_rows, "req", axis=0, tiled=True),
        weight_rows,
        preferred_element_type=jnp.float32,
    )
    mixed = lax.psum(partial_mix.astype(jnp.bfloat16), "kv").astype(jnp.float32)
    middle = residual_in.astype(jnp.float32) + mixed
    scaled = (middle * mlp_gain).astype(jnp.bfloat16)
    squares = jnp.sum(middle * middle, axis=-1)
    gate_part = jnp.dot(scaled, gate_weight, preferred_element_type=jnp.float32)
    upper_part = jnp.dot(scaled, up_weight, preferred_element_type=jnp.float32)
    gate_total, upper_total, square_total = (
        lax.psum(gate_part.astype(jnp.bfloat16), "req").astype(jnp.float32),
        lax.psum(upper_part.astype(jnp.bfloat16), "req").astype(jnp.float32),
        lax.psum(squares.astype(jnp.bfloat16), "req").astype(jnp.float32),
    )
    inverse = (1.0 / jnp.sqrt(square_total / MODEL_WIDTH + EPS))[:, None]
    hidden = (jax.nn.silu(gate_total * inverse) * (upper_total * inverse)).astype(jnp.bfloat16)
    partial_out = jnp.dot(hidden, down_weight, preferred_element_type=jnp.float32)
    summed = lax.psum_scatter(
        partial_out.astype(jnp.bfloat16), "kv", scatter_dimension=0, tiled=True
    ).astype(jnp.float32)
    share = summed.shape[0]
    base_rows = lax.dynamic_slice_in_dim(middle, kv_place * share, share, 0)
    return (base_rows + summed).astype(jnp.bfloat16)


def solution(mesh):
    return jax.shard_map(
        shards,
        mesh=mesh,
        in_specs=(
            P(None, "req"),
            P(),
            P(None, "kv"),
            P(None, "kv"),
            P(None, "kv"),
            P("req", "kv", None, None),
            P("req", "kv", None, None),
            P("req"),
            P("req"),
            P(None, "req"),
            P("req"),
            P("req", "kv"),
            P("req", "kv"),
            P("kv", "req"),
        ),
        out_specs=P("kv", "req"),
        check_vma=False,
    )
```

profile of v0, /device:TPU:0, one launch (start us, length us, event | category | flops | bytes accessed | tf_op | source)
XLA Modules:
  0.0 266.5 jit_solution(15984500769440598371)
XLA Ops:
  6.5 8.1 %all-to-all-start = ((bf16[16,32,256]{2,1,0:T(8,128)(2,1)}), bf16[16,32,256]{2,1,0:T(8,128)(2,1)S(1)}, u32[]{:S(2)}, u32[]{:S(2)}) async-start(bf16[16,32,256]{2,1,0:T(8,128)(2,1)} %bitcast.48), calls=%async_computation | async-start | bytes 524288 | tf_op jit(solution)/shard_map/all_to_all | solution.py:66
  14.7 0.7 broadcast_add_fusion
  15.4 0.7 fusion.29
  16.1 0.7 mul.176
  16.9 6.4 %copy.30 = bf16[512,4096]{1,0:T(8,128)(2,1)} copy(bf16[512,4096]{0,1:T(8,128)(2,1)} %bitcast.49) | data formatting | bytes 8388608 | tf_op jit(solution)/shard_map/dot_general | solution.py:77
  23.5 0.2 fusion.19
  24.2 1.7 convolution_bitcast_fusion
  26.1 0.5 copy-done.1
  26.6 1.3 fusion.51
  28.4 1.8 fusion.50
  30.2 0.3 fusion.24
  30.6 0.3 fusion.18
  30.9 3.6 %fusion.12 = bf16[32,4,128]{2,1,0:T(4,128)(2,1)S(1)} fusion(bf16[32,1,640,128]{3,2,1,0:T(8,128)(2,1)} %param.20, f32[32,4,640]{2,1,0:T(4,128)S(1)} %get-tuple-element.18, f32[32,4]{1,0:T(8,128)S(1)} %get-tuple-element.12, f32[32,4]{1,0:T(8,128)S(1)} %multiply_maximum_fusion, pred[32,640]{1,0:T(8,128)(4,1)S(1)} %fusion.29, f32[32,128]{1,0:T(8,128)S(1)} %fusion.18, ...), kind=kOutput, calls=%fused_computation.12 | convolution fusion | flops 21348352 | bytes 5641728 | tf_op jit(solution)/shard_map/bgj,bjd->bgd/dot_general | solution.py:42
  34.5 24.4 %all_gather.3 = bf16[512,512]{1,0:T(8,128)(2,1)S(1)} all-gather(bf16[32,512]{1,0:T(8,128)(2,1)S(1)} %bitcast.52), channel_id=1, replica_groups=mesh['req'=16,'kv'=8] {'req'}, dimensions={0}, use_global_device_ids=true | all-gather | bytes 557056 | tf_op jit(solution)/shard_map/all_gather | solution.py:114
  58.9 1.0 convolution_convert_fusion.2
  60.0 59.4 %all-reduce.4.cloned.1.call-done = bf16[512,256]{1,0:T(8,128)(2,1)} async-done(((bf16[512,256]{1,0:T(8,128)(2,1)}), bf16[512,256]{1,0:T(8,128)(2,1)}) %all-reduce.4.cloned.1.call-update) | async-done | bytes 262160 | tf_op jit(solution)/shard_map/psum | solution.py:118
  119.4 2.9 %convolution_convert_fusion = bf16[512,1792]{1,0:T(8,128)(2,1)} fusion(bf16[256,1792]{1,0:T(8,128)(2,1)S(1)} %copy-done.5, f32[256]{0:T(256)S(1)} %copy-done.8, bf16[512,256]{1,0:T(8,128)(2,1)} %all-reduce.4.cloned.1.call-done, bf16[512,256]{1,0:T(8,128)(2,1)S(1)} %copy-done.3), kind=kOutput, calls=%fused_computation.5 | convolution fusion | flops 471334912 | bytes 3277824 | tf_op jit(solution)/shard_map/dot_general | solution.py:123
  122.4 2.9 %convolution_convert_fusion.1 = bf16[512,1792]{1,0:T(8,128)(2,1)} fusion(bf16[256,1792]{1,0:T(8,128)(2,1)S(1)} %copy-done.6, f32[256]{0:T(256)S(1)} %copy-done.8, bf16[512,256]{1,0:T(8,128)(2,1)} %all-reduce.4.cloned.1.call-done, bf16[512,256]{1,0:T(8,128)(2,1)S(1)} %copy-done.3), kind=kOutput, calls=%fused_computation.6 | convolution fusion | flops 471334912 | bytes 3277824 | tf_op jit(solution)/shard_map/dot_general | solution.py:122
  125.4 0.2 convert_add_fusion
  125.5 41.1 %psum.30 = bf16[512]{0:T(512)(128)(2,1)S(1)} all-reduce(bf16[512]{0:T(512)(128)(2,1)S(1)} %get-tuple-element.8), channel_id=1, replica_groups=mesh['req'=16,'kv'=8] {'req'}, use_global_device_ids=true, to_apply=%region_6.7 | all-reduce | flops 512 | bytes 2048 | tf_op jit(solution)/shard_map/psum | solution.py:127
  166.7 57.5 %all-reduce.6.cloned.1.call-done = (bf16[512,1792]{1,0:T(8,128)(2,1)}, bf16[512,1792]{1,0:T(8,128)(2,1)}) async-done(((bf16[512,1792]{1,0:T(8,128)(2,1)}, bf16[512,1792]{1,0:T(8,128)(2,1)}), (bf16[512,1792]{1,0:T(8,128)(2,1)}, bf16[512,1792]{1,0:T(8,128)(2,1)})) %all-reduce.6.cloned.1.call-update) | async-done | bytes 3670032 | tf_op jit(solution)/shard_map/psum | solution.py:126
  224.2 4.4 %fusion.5 = bf16[512,256]{1,0:T(8,128)(2,1)} fusion(bf16[1792,256]{1,0:T(8,128)(2,1)} %param.27, bf16[512,1792]{1,0:T(8,128)(2,1)} %get-tuple-element.5, bf16[512,1792]{1,0:T(8,128)(2,1)} %get-tuple-element.6, f32[512]{0:T(512)S(1)} %add_rsqrt_fusion), kind=kOutput, calls=%fused_computation.9 | convolution fusion | flops 479068160 | bytes 4851712 | tf_op jit(solution)/shard_map/dot_general | solution.py:131
  228.6 30.0 %reduce-scatter.2.cloned.1.call-done = bf16[64,256]{1,0:T(8,128)(2,1)} async-done(((bf16[512,256]{1,0:T(8,128)(2,1)}), bf16[64,256]{1,0:T(8,128)(2,1)}) %reduce-scatter.2.cloned.1.call-update) | async-done | bytes 32784 | tf_op jit(solution)/shard_map/reduce_scatter | solution.py:132
  258.6 1.4 add_convert_fusion
  (47 shorter events, 1.5 us)
Async XLA Ops:
  6.5 52.4 %copy-start = (bf16[4096,256]{1,0:T(8,128)(2,1)S(1)}, bf16[4096,256]{1,0:T(8,128)(2,1)}, u32[]{:S(2)}) copy-start(bf16[4096,256]{1,0:T(8,128)(2,1)} %param.23) | copy-start | bytes 6291460
  6.5 16.9 %all-to-all-start = ((bf16[16,32,256]{2,1,0:T(8,128)(2,1)}), bf16[16,32,256]{2,1,0:T(8,128)(2,1)S(1)}, u32[]{:S(2)}, u32[]{:S(2)}) async-start(bf16[16,32,256]{2,1,0:T(8,128)(2,1)} %bitcast.48), calls=%async_computation | async-start | bytes 524288 | tf_op jit(solution)/shard_map/all_to_all | solution.py:66
  14.6 104.8 %all-reduce.4.cloned.1.call-start = ((), (), s32[]{:S(2)}) async-start(), calls=%async_computation.2 | async-start | bytes 524288 | tf_op jit(solution)/shard_map/psum | solution.py:118
  16.9 6.5 %copy-start.10 = (s32[32]{0:T(128)S(1)}, s32[32]{0:T(128)}, u32[]{:S(2)}) copy-start(s32[32]{0:T(128)} %param.22) | copy-start | bytes 388
  23.3 0.9 copy-start.7
  24.1 2.5 copy-start.1
  24.2 4.2 %copy-start.2 = (bf16[32,1,640,128]{3,2,1,0:T(8,128)(2,1)S(1)}, bf16[32,1,640,128]{3,2,1,0:T(8,128)(2,1)}, u32[]{:S(2)}) copy-start(bf16[32,1,640,128]{3,2,1,0:T(8,128)(2,1)} %param.19) | copy-start | bytes 15728644
  27.9 2.6 copy-start.9
  30.9 88.5 %copy-start.3 = (bf16[512,256]{1,0:T(8,128)(2,1)S(1)}, bf16[512,256]{1,0:T(8,128)(2,1)}, u32[]{:S(2)}) copy-start(bf16[512,256]{1,0:T(8,128)(2,1)} %param.14) | copy-start | bytes 786436
  30.9 88.5 %copy-start.5 = (bf16[256,1792]{1,0:T(8,128)(2,1)S(1)}, bf16[256,1792]{1,0:T(8,128)(2,1)}, u32[]{:S(2)}) copy-start(bf16[256,1792]{1,0:T(8,128)(2,1)} %param.26) | copy-start | bytes 2752516
  30.9 88.5 %copy-start.8 = (f32[256]{0:T(256)S(1)}, f32[256]{0:T(256)}, u32[]{:S(2)}) copy-start(f32[256]{0:T(256)} %param.24) | copy-start | bytes 3076
  60.0 164.2 %all-reduce.6.cloned.1.call-start = ((), (), s32[]{:S(2)}) async-start(), calls=%async_computation.4 | async-start | bytes 7340032 | tf_op jit(solution)/shard_map/psum | solution.py:126
  119.4 3.0 %copy-start.6 = (bf16[256,1792]{1,0:T(8,128)(2,1)S(1)}, bf16[256,1792]{1,0:T(8,128)(2,1)}, u32[]{:S(2)}) copy-start(bf16[256,1792]{1,0:T(8,128)(2,1)} %param.25) | copy-start | bytes 2752516
  122.4 3.0 %copy-start.4 = (bf16[512,256]{1,0:T(8,128)(2,1)S(1)}, bf16[512,256]{1,0:T(8,128)(2,1)}, u32[]{:S(2)}) copy-start(bf16[512,256]{1,0:T(8,128)(2,1)} %all-reduce.4.cloned.1.call-done) | copy-start | bytes 786436
  125.3 133.3 %reduce-scatter.2.cloned.1.call-start = ((), (), s32[]{:S(2)}) async-start(), calls=%async_computation.3 | async-start | bytes 294912 | tf_op jit(solution)/shard_map/reduce_scatter | solution.py:132
Sparse Core Ops, SparseCore 0:
  60.1 59.2 all-reduce.3
  125.4 98.6 all-reduce.5
  228.8 29.7 reduce-scatter.1
where the time goes:
time: 267 us; the launch traced here: 266 us
  waiting for transfers between devices  147 us (55%)
  blocking collectives  65.5 us (25%)
  matrix products  20.2 us (8%)
  between operations  13.4 us (5%)
  starting transfers between devices  8.22 us (3%)
  local copies, waits for them, and re-layouts  8.06 us (3%)
  other arithmetic  4.23 us (2%)
    psum x1, waiting for transfers between devices, shards(): mixed = lax.psum(partial_mix.astype(jnp.bfloat16), 'kv').astype(jnp.float32)  59.4 us
    psum x1, waiting for transfers between devices, shards(): lax.psum(upper_part.astype(jnp.bfloat16), 'req').astype(jnp.float32)  57.5 us
    psum x1, blocking collectives, shards(): lax.psum(squares.astype(jnp.bfloat16), 'req').astype(jnp.float32)  41.1 us
    reduce_scatter x1, waiting for transfers between devices, shards(): lax.psum_scatter(partial_out.astype(jnp.bfloat16), 'kv', scatter_dimensio...  30 us
    all_gather x1, blocking collectives, shards(): lax.all_gather(attended_rows, 'req', axis=0, tiled=True)  24.4 us
    all_to_all x1, starting transfers between devices, shards(): lax.all_to_all(residual_in, 'req', split_axis=0, concat_axis=1, tiled=True)  8.09 us
    dot_general x1, local copies, waits for them, and re-layouts, shards(): jnp.dot(normed_input, query_weight, preferred_element_type=jnp.float32)  6.45 us
  transfers between devices with their start and end apart: 4, of which 3 were waited for; matrix products, arithmetic and copies ran while one was open for 3% of the time, Pallas kernels for 0%

commit v1 on v0

--- a/solution.py
+++ b/solution.py
@@ -123,7 +123,7 @@
     upper_part = jnp.dot(scaled, up_weight, preferred_element_type=jnp.float32)
     gate_total, upper_total, square_total = (
         lax.psum(gate_part.astype(jnp.bfloat16), "req").astype(jnp.float32),
-        lax.psum(upper_part.astype(jnp.bfloat16), "req").astype(jnp.float32),
+        jnp.sum(lax.all_gather(upper_part.astype(jnp.bfloat16), "req"), axis=0).astype(jnp.float32),
         lax.psum(squares.astype(jnp.bfloat16), "req").astype(jnp.float32),
     )
     inverse = (1.0 / jnp.sqrt(square_total / MODEL_WIDTH + EPS))[:, None]

time: 267 us -> 434 us (1.63)
  waiting for transfers between devices: 147 us -> 301 us
  other arithmetic: 4.23 us -> 16.1 us
    all_gather x0 -> x1, waiting for transfers between devices: none -> 131 us  [shards(): lax.all_gather(upper_part.astype(jnp.bfloat16), 'req')]
    psum x1, waiting for transfers between devices: 57.5 us -> 81.1 us  [shards(): lax.psum(gate_part.astype(jnp.bfloat16), 'req').astype(jnp.float32)]
    reduce_sum x0 -> x1, other arithmetic: none -> 11.9 us  [shards(): jnp.sum(lax.all_gather(upper_part.astype(jnp.bfloat16), 'req'), axis=0)]
  transfers between devices with their start and end apart: 4 -> 5, of which waited for: 3 -> 4; matrix products, arithmetic and copies ran while one was open for 3% -> 6% of each run, Pallas kernels for 0% -> 0%
where the time goes in v1:
time: 434 us; the launch traced here: 433 us
  waiting for transfers between devices  301 us (69%)
  blocking collectives  65.6 us (15%)
  matrix products  20.5 us (5%)
  other arithmetic  16.1 us (4%)
  between operations  13.4 us (3%)
  starting transfers between devices  8.26 us (2%)
  local copies, waits for them, and re-layouts  8.03 us (2%)
    all_gather x1, waiting for transfers between devices, shards(): lax.all_gather(upper_part.astype(jnp.bfloat16), 'req')  131 us
    psum x1, waiting for transfers between devices, shards(): lax.psum(gate_part.astype(jnp.bfloat16), 'req').astype(jnp.float32)  81.1 us
    psum x1, waiting for transfers between devices, shards(): mixed = lax.psum(partial_mix.astype(jnp.bfloat16), 'kv').astype(jnp.float32)  59.4 us
    psum x1, blocking collectives, shards(): lax.psum(squares.astype(jnp.bfloat16), 'req').astype(jnp.float32)  41.2 us
    reduce_scatter x1, waiting for transfers between devices, shards(): lax.psum_scatter(partial_out.astype(jnp.bfloat16), 'kv', scatter_dimensio...  29.9 us
    all_gather x1, blocking collectives, shards(): lax.all_gather(attended_rows, 'req', axis=0, tiled=True)  24.4 us
    reduce_sum x1, other arithmetic, shards(): jnp.sum(lax.all_gather(upper_part.astype(jnp.bfloat16), 'req'), axis=0)  11.9 us
  transfers between devices with their start and end apart: 5, of which 4 were waited for; matrix products, arithmetic and copies ran while one was open for 6% of the time, Pallas kernels for 0%

profile of v1, /device:TPU:0, one launch (start us, length us, event | category | flops | bytes accessed | tf_op | source)
XLA Modules:
  0.0 433.0 jit_solution(164147304556570544)
XLA Ops:
  6.5 8.1 %all-to-all-start = ((bf16[16,32,256]{2,1,0:T(8,128)(2,1)}), bf16[16,32,256]{2,1,0:T(8,128)(2,1)S(1)}, u32[]{:S(2)}, u32[]{:S(2)}) async-start(bf16[16,32,256]{2,1,0:T(8,128)(2,1)} %bitcast.50), calls=%async_computation | async-start | bytes 524288 | tf_op jit(solution)/shard_map/all_to_all | solution.py:66
  14.7 0.7 broadcast_add_fusion
  15.4 0.7 fusion.29
  16.1 0.7 mul.176
  16.9 6.4 %copy.30 = bf16[512,4096]{1,0:T(8,128)(2,1)} copy(bf16[512,4096]{0,1:T(8,128)(2,1)} %bitcast.51) | data formatting | bytes 8388608 | tf_op jit(solution)/shard_map/dot_general | solution.py:77
  24.2 1.7 convolution_bitcast_fusion
  26.1 0.5 copy-done.2
  26.6 1.3 fusion.51
  28.4 1.8 fusion.50
  30.2 0.3 fusion.24
  30.5 0.3 fusion.18
  30.9 3.6 fusion.12
  34.5 24.4 %all_gather.9 = bf16[512,512]{1,0:T(8,128)(2,1)S(1)} all-gather(bf16[32,512]{1,0:T(8,128)(2,1)S(1)} %bitcast.54), channel_id=1, replica_groups=mesh['req'=16,'kv'=8] {'req'}, dimensions={0}, use_global_device_ids=true | all-gather | bytes 557056 | tf_op jit(solution)/shard_map/all_gather | solution.py:114
  58.9 1.0 convolution_convert_fusion.2
  60.0 59.4 %all-reduce.3.cloned.1.call-done = bf16[512,256]{1,0:T(8,128)(2,1)} async-done(((bf16[512,256]{1,0:T(8,128)(2,1)}), bf16[512,256]{1,0:T(8,128)(2,1)}) %all-reduce.3.cloned.1.call-update) | async-done | bytes 262160 | tf_op jit(solution)/shard_map/psum | solution.py:118
  119.4 2.9 convolution_convert_fusion
  122.4 3.1 convolution_convert_fusion.1
  125.7 41.2 %psum.23 = bf16[512]{0:T(512)(128)(2,1)S(1)} all-reduce(bf16[512]{0:T(512)(128)(2,1)S(1)} %get-tuple-element.6), channel_id=1, replica_groups=mesh['req'=16,'kv'=8] {'req'}, use_global_device_ids=true, to_apply=%region_6.7 | all-reduce | flops 512 | bytes 2048 | tf_op jit(solution)/shard_map/psum | solution.py:127
  166.9 130.7 %all-gather.3.cloned.1.call-done = bf16[8192,1792]{1,0:T(8,128)(2,1)} async-done(((bf16[512,1792]{1,0:T(8,128)(2,1)}), bf16[8192,1792]{1,0:T(8,128)(2,1)}) %all-gather.3.cloned.1.call-update) | async-done | bytes 29360144 | tf_op jit(solution)/shard_map/all_gather | solution.py:126
  297.6 11.9 %reduce_sum.42 = bf16[512,1792]{1,0:T(8,128)(2,1)} reduce(bf16[16,512,1792]{2,1,0:T(8,128)(2,1)} %bitcast.48, bf16[]{:T(256)} %constant.41.clone.1), dimensions={0}, to_apply=%region_7.8 | reduce | flops 13762560 | bytes 31195138 | tf_op jit(solution)/shard_map/reduce_sum | solution.py:126
  309.5 81.1 %all-reduce.5.cloned.1.call-done = bf16[512,1792]{1,0:T(8,128)(2,1)} async-done(((bf16[512,1792]{1,0:T(8,128)(2,1)}), bf16[512,1792]{1,0:T(8,128)(2,1)}) %all-reduce.5.cloned.1.call-update) | async-done | bytes 1835024 | tf_op jit(solution)/shard_map/psum | solution.py:125
  390.6 4.6 %fusion.5 = bf16[512,256]{1,0:T(8,128)(2,1)} fusion(bf16[1792,256]{1,0:T(8,128)(2,1)} %param.27, bf16[512,1792]{1,0:T(8,128)(2,1)} %reduce_sum.42, bf16[512,1792]{1,0:T(8,128)(2,1)} %all-reduce.5.cloned.1.call-done, f32[512]{0:T(512)S(1)} %add_rsqrt_fusion), kind=kOutput, calls=%fused_computation.9 | convolution fusion | flops 479068160 | bytes 4851712 | tf_op jit(solution)/shard_map/dot_general | solution.py:131
  395.2 29.9 %reduce-scatter.2.cloned.1.call-done = bf16[64,256]{1,0:T(8,128)(2,1)} async-done(((bf16[512,256]{1,0:T(8,128)(2,1)}), bf16[64,256]{1,0:T(8,128)(2,1)}) %reduce-scatter.2.cloned.1.call-update) | async-done | bytes 32784 | tf_op jit(solution)/shard_map/reduce_scatter | solution.py:132
  425.1 1.4 add_convert_fusion
  (51 shorter events, 1.9 us)
Async XLA Ops:
  6.5 52.4 %copy-start = (bf16[4096,256]{1,0:T(8,128)(2,1)S(1)}, bf16[4096,256]{1,0:T(8,128)(2,1)}, u32[]{:S(2)}) copy-start(bf16[4096,256]{1,0:T(8,128)(2,1)} %param.23) | copy-start | bytes 6291460
  6.5 16.9 %all-to-all-start = ((bf16[16,32,256]{2,1,0:T(8,128)(2,1)}), bf16[16,32,256]{2,1,0:T(8,128)(2,1)S(1)}, u32[]{:S(2)}, u32[]{:S(2)}) async-start(bf16[16,32,256]{2,1,0:T(8,128)(2,1)} %bitcast.50), calls=%async_computation | async-start | bytes 524288 | tf_op jit(solution)/shard_map/all_to_all | solution.py:66
  14.6 104.7 %all-reduce.3.cloned.1.call-start = ((), (), s32[]{:S(2)}) async-start(), calls=%async_computation.2 | async-start | bytes 524288 | tf_op jit(solution)/shard_map/psum | solution.py:118
  16.9 6.4 %copy-start.10 = (s32[32]{0:T(128)S(1)}, s32[32]{0:T(128)}, u32[]{:S(2)}) copy-start(s32[32]{0:T(128)} %param.22) | copy-start | bytes 388
  23.3 0.9 copy-start.7
  24.1 2.5 copy-start.2
  24.2 4.2 copy-start.3
  27.9 2.6 copy-start.9
  30.9 88.5 %copy-start.4 = (bf16[512,256]{1,0:T(8,128)(2,1)S(1)}, bf16[512,256]{1,0:T(8,128)(2,1)}, u32[]{:S(2)}) copy-start(bf16[512,256]{1,0:T(8,128)(2,1)} %param.14) | copy-start | bytes 786436
  30.9 88.5 %copy-start.6 = (bf16[256,1792]{1,0:T(8,128)(2,1)S(1)}, bf16[256,1792]{1,0:T(8,128)(2,1)}, u32[]{:S(2)}) copy-start(bf16[256,1792]{1,0:T(8,128)(2,1)} %param.26) | copy-start | bytes 2752516
  30.9 88.4 %copy-start.8 = (f32[256]{0:T(256)S(1)}, f32[256]{0:T(256)}, u32[]{:S(2)}) copy-start(f32[256]{0:T(256)} %param.24) | copy-start | bytes 3076
  59.9 237.7 %all-gather.3.cloned.1.call-start = ((), (), s32[]{:S(2)}) async-start(), calls=%async_computation.5 | async-start | bytes 31195136 | tf_op jit(solution)/shard_map/all_gather | solution.py:126
  119.4 3.0 copy-start.5
  122.3 268.3 %all-reduce.5.cloned.1.call-start = ((), (), s32[]{:S(2)}) async-start(), calls=%async_computation.3 | async-start | bytes 3670016 | tf_op jit(solution)/shard_map/psum | solution.py:125
  125.5 299.6 %reduce-scatter.2.cloned.1.call-start = ((), (), s32[]{:S(2)}) async-start(), calls=%async_computation.4 | async-start | bytes 294912 | tf_op jit(solution)/shard_map/reduce_scatter | solution.py:132
  390.6 35.9 %copy-start.1 = (bf16[4096,256]{1,0:T(8,128)(2,1)S(1)}, bf16[4096,256]{1,0:T(8,128)(2,1)}, u32[]{:S(2)}) copy-start(bf16[4096,256]{1,0:T(8,128)(2,1)} %param.23) | copy-start | bytes 6291460
Sparse Core Ops, SparseCore 0:
  60.0 59.2 all-reduce.2
  122.4 175.1 all-gather.2
  301.3 89.2 all-reduce.4
  395.3 29.7 reduce-scatter.1
